TPU v7x, 128 devices: a whole 4x4x4 slice. The times are simulated.
128 devices in a mesh: mem: 8 (over z_lo, y), sp: 16 (over z_hi, x, core).
Axes of the slice: x: 4, y: 4, z: 4 (z_hi: 2, z_lo: 2; z = z_hi * 2 + z_lo), core: 2. Of those that a mesh axis runs over, the one named last changes fastest.
Arguments:
- anomalies: float32 [64, 3, 256, 4096], P('mem', None, 'sp'), may hold values from -6 to 6
- mean_state: float32 [3, 256, 4096], P(None, 'sp'), may hold values from -3 to 3
- weights: float32 [64], replicated, may hold values from -0.4375 to 0.4375
- station_row: int32 [4096], P('sp'), may hold values from 0 to 14
- station_col: int32 [4096], P('sp'), may hold values from 0 to 4095
- stencil_row: int32 [4, 4096], P(None, 'sp'), may hold values from 0 to 1
- stencil_col: int32 [4, 4096], P(None, 'sp'), may hold values from -1 to 1
- obs_weight: float32 [4, 4096], P(None, 'sp'), may hold values from 0.05 to 0.25
- obs_value: float32 [4, 4096], P(None, 'sp'), may hold values from -6 to 6
- obs_var: float32 [4, 4096], P(None, 'sp'), may hold values from 1 to 10
Outputs:
- obs_anom: float32 [64, 4, 4096], P('mem', None, 'sp')
- gradient: float32 [64], replicated
- hessian: float32 [64, 64], replicated
All inputs are finite; a program needn't handle non-finite values.
Results may differ from a plain program's by a relative error of at most 0.0003.
Values sent between devices are 32-bit elements; how exact they have to be, the bound alone decides.
No kernel may reach another device: no remote copies, remote signals or barrier semaphores. Data moves between devices by JAX's collectives and lax.ppermute only.
A program may use at most 192 MiB of HBM per device.

v0:
```python
import jax
import jax.numpy as jnp
from jax import lax
from jax.sharding import PartitionSpec as P

STEPS = 4
time_step = 1.0
coriolis = 0.1
perturb = 0.1


def padded_2(block, sides, width):
    for axis, dim in sides:
        count = lax.axis_size(axis)
        forward = [(i, i + 1) for i in range(count - 1)]
        forward.append((count - 1, 0))
        backward = [(target, source) for source, target in forward]
        low = lax.ppermute(
            lax.slice_in_dim(block, block.shape[dim] - width, None, axis=dim), axis, forward
        )
        high = lax.ppermute(lax.slice_in_dim(block, 0, width, axis=dim), axis, backward)
        block = jnp.concatenate([low, block, high], axis=dim)
    return block


def row_diff(a):
    return (a[:, 2:] - a[:, :-2]) * 0.5


def col_diff(a):
    return (jnp.roll(a, -1, axis=-1) - jnp.roll(a, 1, axis=-1)) * 0.5


def height_update(height, along, across):
    depth = 1.0 + height
    return height[:, 1:-1] - time_step * (
        row_diff(depth * along) + col_diff(depth * across)[:, 1:-1]
    )


def momentum_update(fresh, along, across):
    inner_u = along[:, 1:-1]
    inner_v = across[:, 1:-1]
    new_u = inner_u + time_step * (
        coriolis * inner_v
        - row_diff(fresh)
        - inner_u * row_diff(along)
        - inner_v * col_diff(along)[:, 1:-1]
    )
    new_v = inner_v + time_step * (
        -coriolis * inner_u
        - col_diff(fresh)[:, 1:-1]
        - inner_u * row_diff(across)
        - inner_v * col_diff(across)[:, 1:-1]
    )
    return jnp.stack([fresh[:, 1:-1], new_u, new_v], axis=1)


def observe(height, flat_index, obs_weight):
    flat = height.reshape(height.shape[0], -1)
    picked = jnp.take(flat, flat_index, axis=1)
    return jnp.sum(obs_weight[None] * picked, axis=1)


def body(
    anomalies,
    mean_state,
    weights,
    station_row,
    station_col,
    stencil_row,
    stencil_col,
    obs_weight,
    obs_value,
    obs_var,
):
    members = anomalies.shape[0]
    columns = anomalies.shape[3]
    total = weights.shape[0]
    first = lax.axis_index("mem") * members
    own_weights = lax.dynamic_slice_in_dim(weights, first, members, 0)
    partial_value = jnp.tensordot(own_weights, anomalies, axes=1, precision=lax.Precision.HIGHEST)
    increment = lax.psum(partial_value, "mem")
    centre = mean_state + increment
    state = centre[None] + perturb * anomalies
    flat_index = (station_row[None, :] + stencil_row) * columns + (
        station_col[None, :] + stencil_col
    ) % columns
    seen = []
    for step in range(STEPS):
        padded = padded_2(state, (("sp", 2),), 1)
        fresh = height_update(padded[:, 0], padded[:, 1], padded[:, 2])
        fresh_pad = padded_2(fresh, (("sp", 1),), 1)
        state = momentum_update(fresh_pad, padded[:, 1], padded[:, 2])
        seen.append(observe(state[:, 0], flat_index, obs_weight))
    own_obs = jnp.stack(seen, axis=1)
    gathered = lax.all_gather(own_obs, "mem", axis=0, tiled=True)
    mean_obs = jnp.mean(gathered, axis=0)
    obs_anom = (own_obs - mean_obs) / perturb
    flat_anom = ((gathered - mean_obs) / perturb).reshape(total, -1)
    weighted = flat_anom * (1.0 / obs_var).reshape(-1)
    innov = (obs_value - mean_obs).reshape(-1)
    gram = jnp.dot(weighted, flat_anom.T, precision=lax.Precision.HIGHEST)
    pull = jnp.dot(weighted, innov, precision=lax.Precision.HIGHEST)
    gram, pull = lax.psum((gram, pull), "sp")
    hessian = gram + (total - 1) * jnp.eye(total, dtype=jnp.float32)
    gradient = (total - 1) * weights - pull
    return (obs_anom, gradient, hessian)


def solution(mesh):
    return jax.shard_map(
        body,
        mesh=mesh,
        in_specs=(
            P("mem", None, "sp", None),
            P(None, "sp", None),
            P(),
            P("sp"),
            P("sp"),
            P(None, "sp"),
            P(None, "sp"),
            P(None, "sp"),
            P(None, "sp"),
            P(None, "sp"),
        ),
        out_specs=(P("mem", None, "sp"), P(), P()),
        check_vma=False,
    )
```

profile of v0, /device:TPU:0, one launch (start us, length us, event | category | flops | bytes accessed | tf_op | source)
XLA Modules:
  0.0 450.2 jit_solution(12270124455747146730)
XLA Ops:
  7.2 11.4 %fusion = f32[1,3,16,4096]{3,0,2,1:T(1,128)S(1)} fusion(f32[8,3,16,4096]{3,2,1,0:T(8,128)} %param.12, f32[64]{0:T(128)} %param.14, s32[]{:T(128)S(6)} %select_n.17), kind=kOutput, calls=%fused_computation.9 | convolution fusion | flops 18874368 | bytes 7078148 | tf_op jit(solution)/shard_map/dot_general | solution.py:82
  20.0 78.6 %all-reduce.3.cloned.1.call-done = f32[3,16,4096]{2,1,0:T(8,128)} async-done(((f32[3,16,4096]{2,1,0:T(8,128)}), f32[3,16,4096]{2,1,0:T(8,128)}) %all-reduce.3.cloned.1.call-update) | async-done | bytes 786448 | tf_op jit(solution)/shard_map/psum | solution.py:83
  99.8 7.0 %multiply_add_fusion = f32[8,3,16,4096]{3,0,2,1:T(8,128)S(1)} fusion(f32[8,3,16,4096]{3,2,1,0:T(8,128)} %param.12, f32[3,16,4096]{2,1,0:T(8,128)S(1)} %add.97), kind=kLoop, calls=%fused_computation.8 | loop fusion | flops 3145728 | bytes 13369344 | tf_op jit(solution)/shard_map/add | solution.py:85
  106.9 5.5 %collective-permute-start.1 = (f32[8,3,1,4096]{3,0,2,1:T(8,128)S(1)}, f32[8,3,1,4096]{3,0,2,1:T(8,128)S(1)}, u32[]{:S(2)}, u32[]{:S(2)}) collective-permute-start(f32[8,3,1,4096]{3,0,2,1:T(8,128)S(1)} %get-tuple-element.42), channel_id=1, source_target_pairs={{1,0},{2,1},{3,2},{4,3},{5,4},{6,5},{7,6},{8,7},{9,8},{10,9},{11,1... | collective-permute-start | bytes 1179656 | tf_op jit(solution)/shard_map/ppermute | solution.py:21
  112.4 5.3 %collective-permute-done = f32[8,3,1,4096]{3,0,2,1:T(8,128)S(1)} collective-permute-done((f32[8,3,1,4096]{3,0,2,1:T(8,128)S(1)}, f32[8,3,1,4096]{3,0,2,1:T(8,128)S(1)}, u32[]{:S(2)}, u32[]{:S(2)}) %collective-permute-start) | collective-permute-done | bytes 393248 | tf_op jit(solution)/shard_map/ppermute | solution.py:18
  121.3 5.6 %collective-permute-start.2 = (f32[8,1,4096]{2,0,1:T(8,128)S(1)}, f32[8,1,4096]{2,0,1:T(8,128)S(1)}, u32[]{:S(2)}, u32[]{:S(2)}) collective-permute-start(f32[8,1,4096]{2,0,1:T(8,128)S(1)} %get-tuple-element.94), channel_id=1, source_target_pairs={{1,0},{2,1},{3,2},{4,3},{5,4},{6,5},{7,6},{8,7},{9,8},{10,9},{11,1... | collective-permute-start | bytes 393224 | tf_op jit(solution)/shard_map/ppermute | solution.py:21
  141.9 5.5 %collective-permute-start.5 = (f32[8,3,1,4096]{3,0,2,1:T(8,128)S(1)}, f32[8,3,1,4096]{3,0,2,1:T(8,128)S(1)}, u32[]{:S(2)}, u32[]{:S(2)}) collective-permute-start(f32[8,3,1,4096]{3,0,2,1:T(8,128)S(1)} %get-tuple-element.40), channel_id=1, source_target_pairs={{1,0},{2,1},{3,2},{4,3},{5,4},{6,5},{7,6},{8,7},{9,8},{10,9},{11,1... | collective-permute-start | bytes 1179656 | tf_op jit(solution)/shard_map/ppermute | solution.py:21
  147.4 5.3 %collective-permute-done.4 = f32[8,3,1,4096]{3,0,2,1:T(8,128)S(1)} collective-permute-done((f32[8,3,1,4096]{3,0,2,1:T(8,128)S(1)}, f32[8,3,1,4096]{3,0,2,1:T(8,128)S(1)}, u32[]{:S(2)}, u32[]{:S(2)}) %collective-permute-start.4) | collective-permute-done | bytes 393248 | tf_op jit(solution)/shard_map/ppermute | solution.py:18
  157.6 5.6 %collective-permute-start.6 = (f32[8,1,4096]{2,0,1:T(8,128)S(1)}, f32[8,1,4096]{2,0,1:T(8,128)S(1)}, u32[]{:S(2)}, u32[]{:S(2)}) collective-permute-start(f32[8,1,4096]{2,0,1:T(8,128)S(1)} %get-tuple-element.92), channel_id=1, source_target_pairs={{1,0},{2,1},{3,2},{4,3},{5,4},{6,5},{7,6},{8,7},{9,8},{10,9},{11,1... | collective-permute-start | bytes 393224 | tf_op jit(solution)/shard_map/ppermute | solution.py:21
  165.7 5.5 %collective-permute-done.7 = f32[8,1,4096]{2,0,1:T(8,128)S(1)} collective-permute-done((f32[8,1,4096]{2,0,1:T(8,128)S(1)}, f32[8,1,4096]{2,0,1:T(8,128)S(1)}, u32[]{:S(2)}, u32[]{:S(2)}) %collective-permute-start.7) | collective-permute-done | bytes 131104 | tf_op jit(solution)/shard_map/ppermute | solution.py:18
  177.4 5.6 %collective-permute-start.9 = (f32[8,3,1,4096]{3,0,2,1:T(8,128)S(1)}, f32[8,3,1,4096]{3,0,2,1:T(8,128)S(1)}, u32[]{:S(2)}, u32[]{:S(2)}) collective-permute-start(f32[8,3,1,4096]{3,0,2,1:T(8,128)S(1)} %get-tuple-element.38), channel_id=1, source_target_pairs={{1,0},{2,1},{3,2},{4,3},{5,4},{6,5},{7,6},{8,7},{9,8},{10,9},{11,1... | collective-permute-start | bytes 1179656 | tf_op jit(solution)/shard_map/ppermute | solution.py:21
  195.2 5.6 %collective-permute-start.10 = (f32[8,1,4096]{2,0,1:T(8,128)S(1)}, f32[8,1,4096]{2,0,1:T(8,128)S(1)}, u32[]{:S(2)}, u32[]{:S(2)}) collective-permute-start(f32[8,1,4096]{2,0,1:T(8,128)S(1)} %get-tuple-element.90), channel_id=1, source_target_pairs={{1,0},{2,1},{3,2},{4,3},{5,4},{6,5},{7,6},{8,7},{9,8},{10,9},{11,1... | collective-permute-start | bytes 393224 | tf_op jit(solution)/shard_map/ppermute | solution.py:21
  203.3 5.5 %collective-permute-done.11 = f32[8,1,4096]{2,0,1:T(8,128)S(1)} collective-permute-done((f32[8,1,4096]{2,0,1:T(8,128)S(1)}, f32[8,1,4096]{2,0,1:T(8,128)S(1)}, u32[]{:S(2)}, u32[]{:S(2)}) %collective-permute-start.11) | collective-permute-done | bytes 131104 | tf_op jit(solution)/shard_map/ppermute | solution.py:18
  216.4 5.6 %collective-permute-start.13 = (f32[8,3,1,4096]{3,0,2,1:T(8,128)}, f32[8,3,1,4096]{3,0,2,1:T(8,128)}, u32[]{:S(2)}, u32[]{:S(2)}) collective-permute-start(f32[8,3,1,4096]{3,0,2,1:T(8,128)} %get-tuple-element.36), channel_id=1, source_target_pairs={{1,0},{2,1},{3,2},{4,3},{5,4},{6,5},{7,6},{8,7},{9,8},{10,9},{11,1... | collective-permute-start | bytes 1179656 | tf_op jit(solution)/shard_map/ppermute | solution.py:21
  222.1 15.6 %copy.29 = f32[8,16,4096]{0,2,1:T(8,128)} copy(f32[8,16,4096]{2,0,1:T(8,128)S(1)} %fusion.94) | data formatting | bytes 4194304 | tf_op jit(solution)/shard_map/sub | solution.py:36
  237.6 13.3 %gather_fusion = f32[1024,8]{1,0:T(8,128)S(1)} fusion(f32[8,65536]{0,1:T(8,128)} %bitcast.122, s32[1024]{0:T(1024)S(1)} %broadcast_clamp_fusion), kind=kCustom, calls=%fused_computation.clone | custom fusion | bytes 69632 | tf_op jit(solution)/shard_map/jit(_take)/gather | solution.py:61
  251.0 16.4 %copy.31 = f32[8,16,4096]{0,2,1:T(8,128)} copy(f32[8,16,4096]{2,0,1:T(8,128)} %copy-done) | data formatting | bytes 4194304 | tf_op jit(solution)/shard_map/sub | solution.py:36
  267.4 13.3 %gather_fusion.1 = f32[1024,8]{1,0:T(8,128)S(1)} fusion(f32[8,65536]{0,1:T(8,128)} %bitcast.123, s32[1024]{0:T(1024)S(1)} %broadcast_clamp_fusion), kind=kCustom, calls=%fused_computation.1.clone | custom fusion | bytes 69632 | tf_op jit(solution)/shard_map/jit(_take)/gather | solution.py:61
  280.8 15.6 %copy.33 = f32[8,16,4096]{0,2,1:T(8,128)} copy(f32[8,16,4096]{2,0,1:T(8,128)S(1)} %copy-done.2) | data formatting | bytes 4194304 | tf_op jit(solution)/shard_map/sub | solution.py:36
  296.3 14.5 %gather_fusion.2 = f32[1024,8]{1,0:T(8,128)} fusion(f32[8,65536]{0,1:T(8,128)} %bitcast.124, s32[1024]{0:T(1024)S(1)} %broadcast_clamp_fusion), kind=kCustom, calls=%fused_computation.2.clone | custom fusion | bytes 69632 | tf_op jit(solution)/shard_map/jit(_take)/gather | solution.py:61
  316.2 15.6 %copy.35 = f32[8,16,4096]{0,2,1:T(8,128)} copy(f32[8,16,4096]{2,0,1:T(8,128)S(1)} %fusion.7) | data formatting | bytes 4194304 | tf_op jit(solution)/shard_map/sub | solution.py:36
  331.8 13.4 %gather_fusion.3 = f32[1024,8]{1,0:T(8,128)S(1)} fusion(f32[8,65536]{0,1:T(8,128)} %bitcast.121, s32[1024]{0:T(1024)S(1)} %broadcast_clamp_fusion), kind=kCustom, calls=%fused_computation.3.clone | custom fusion | bytes 69632 | tf_op jit(solution)/shard_map/jit(_take)/gather | solution.py:61
  346.9 28.4 %all_gather.3 = f32[64,4,256]{2,0,1:T(8,128)S(1)} all-gather(f32[8,4,256]{2,0,1:T(8,128)S(1)} %pad_maximum_fusion.60), channel_id=1, replica_groups=mesh['mem'=8,'sp'=16] {'mem'}, dimensions={0}, use_global_device_ids=true | all-gather | bytes 294912 | tf_op jit(solution)/shard_map/all_gather | solution.py:97
  376.0 65.0 %all-reduce = (f32[64]{0:T(128)S(1)}, f32[64,64]{1,0:T(8,128)S(1)}) all-reduce(f32[64]{0:T(128)S(1)} %convolution_bitcast_fusion.1, f32[64,64]{1,0:T(8,128)S(1)} %convolution_bitcast_fusion), channel_id=1, replica_groups=mesh['mem'=8,'sp'=16] {'sp'}, use_global_device_ids=true, to_apply=%region_6.8 | all-reduce | flops 4160 | bytes 33280 | tf_op jit(solution)/shard_map/psum | solution.py:105
  (124 shorter events, 66.4 us)
Async XLA Ops:
  7.2 91.4 %all-reduce.3.cloned.1.call-start = ((), (), s32[]{:S(2)}) async-start(), calls=%async_computation | async-start | bytes 1572864 | tf_op jit(solution)/shard_map/psum | solution.py:83
  18.6 80.0 %copy-start.7 = (f32[3,16,4096]{2,1,0:T(8,128)S(1)}, f32[3,16,4096]{2,1,0:T(8,128)}, u32[]{:S(2)}) copy-start(f32[3,16,4096]{2,1,0:T(8,128)} %param.13) | copy-start | bytes 2359300
  106.8 10.9 %collective-permute-start = (f32[8,3,1,4096]{3,0,2,1:T(8,128)S(1)}, f32[8,3,1,4096]{3,0,2,1:T(8,128)S(1)}, u32[]{:S(2)}, u32[]{:S(2)}) collective-permute-start(f32[8,3,1,4096]{3,0,2,1:T(8,128)S(1)} %get-tuple-element.41), channel_id=1, source_target_pairs={{0,1},{1,2},{2,3},{3,4},{4,5},{5,6},{6,7},{7,8},{8,9},{9,10},{10,1... | collective-permute-start | bytes 1179656 | tf_op jit(solution)/shard_map/ppermute | solution.py:18
  106.9 10.8 %collective-permute-start.1 = (f32[8,3,1,4096]{3,0,2,1:T(8,128)S(1)}, f32[8,3,1,4096]{3,0,2,1:T(8,128)S(1)}, u32[]{:S(2)}, u32[]{:S(2)}) collective-permute-start(f32[8,3,1,4096]{3,0,2,1:T(8,128)S(1)} %get-tuple-element.42), channel_id=1, source_target_pairs={{1,0},{2,1},{3,2},{4,3},{5,4},{6,5},{7,6},{8,7},{9,8},{10,9},{11,1... | collective-permute-start | bytes 1179656 | tf_op jit(solution)/shard_map/ppermute | solution.py:21
  121.3 8.9 %collective-permute-start.2 = (f32[8,1,4096]{2,0,1:T(8,128)S(1)}, f32[8,1,4096]{2,0,1:T(8,128)S(1)}, u32[]{:S(2)}, u32[]{:S(2)}) collective-permute-start(f32[8,1,4096]{2,0,1:T(8,128)S(1)} %get-tuple-element.94), channel_id=1, source_target_pairs={{1,0},{2,1},{3,2},{4,3},{5,4},{6,5},{7,6},{8,7},{9,8},{10,9},{11,1... | collective-permute-start | bytes 393224 | tf_op jit(solution)/shard_map/ppermute | solution.py:21
  126.8 8.0 %collective-permute-start.3 = (f32[8,1,4096]{2,0,1:T(8,128)S(1)}, f32[8,1,4096]{2,0,1:T(8,128)S(1)}, u32[]{:S(2)}, u32[]{:S(2)}) collective-permute-start(f32[8,1,4096]{2,0,1:T(8,128)S(1)} %get-tuple-element.93), channel_id=1, source_target_pairs={{0,1},{1,2},{2,3},{3,4},{4,5},{5,6},{6,7},{7,8},{8,9},{9,10},{10,1... | collective-permute-start | bytes 393224 | tf_op jit(solution)/shard_map/ppermute | solution.py:18
  141.8 10.9 %collective-permute-start.4 = (f32[8,3,1,4096]{3,0,2,1:T(8,128)S(1)}, f32[8,3,1,4096]{3,0,2,1:T(8,128)S(1)}, u32[]{:S(2)}, u32[]{:S(2)}) collective-permute-start(f32[8,3,1,4096]{3,0,2,1:T(8,128)S(1)} %get-tuple-element.39), channel_id=1, source_target_pairs={{0,1},{1,2},{2,3},{3,4},{4,5},{5,6},{6,7},{7,8},{8,9},{9,10},{10,1... | collective-permute-start | bytes 1179656 | tf_op jit(solution)/shard_map/ppermute | solution.py:18
  141.9 10.8 %collective-permute-start.5 = (f32[8,3,1,4096]{3,0,2,1:T(8,128)S(1)}, f32[8,3,1,4096]{3,0,2,1:T(8,128)S(1)}, u32[]{:S(2)}, u32[]{:S(2)}) collective-permute-start(f32[8,3,1,4096]{3,0,2,1:T(8,128)S(1)} %get-tuple-element.40), channel_id=1, source_target_pairs={{1,0},{2,1},{3,2},{4,3},{5,4},{6,5},{7,6},{8,7},{9,8},{10,9},{11,1... | collective-permute-start | bytes 1179656 | tf_op jit(solution)/shard_map/ppermute | solution.py:21
  157.5 30.8 %copy-start = (f32[8,16,4096]{2,0,1:T(8,128)}, f32[8,16,4096]{2,0,1:T(8,128)S(1)}, u32[]{:S(2)}) copy-start(f32[8,16,4096]{2,0,1:T(8,128)S(1)} %fusion.65) | copy-start | bytes 6291460
  157.6 8.1 %collective-permute-start.6 = (f32[8,1,4096]{2,0,1:T(8,128)S(1)}, f32[8,1,4096]{2,0,1:T(8,128)S(1)}, u32[]{:S(2)}, u32[]{:S(2)}) collective-permute-start(f32[8,1,4096]{2,0,1:T(8,128)S(1)} %get-tuple-element.92), channel_id=1, source_target_pairs={{1,0},{2,1},{3,2},{4,3},{5,4},{6,5},{7,6},{8,7},{9,8},{10,9},{11,1... | collective-permute-start | bytes 393224 | tf_op jit(solution)/shard_map/ppermute | solution.py:21
  163.2 8.0 %collective-permute-start.7 = (f32[8,1,4096]{2,0,1:T(8,128)S(1)}, f32[8,1,4096]{2,0,1:T(8,128)S(1)}, u32[]{:S(2)}, u32[]{:S(2)}) collective-permute-start(f32[8,1,4096]{2,0,1:T(8,128)S(1)} %get-tuple-element.91), channel_id=1, source_target_pairs={{0,1},{1,2},{2,3},{3,4},{4,5},{5,6},{6,7},{7,8},{8,9},{9,10},{10,1... | collective-permute-start | bytes 393224 | tf_op jit(solution)/shard_map/ppermute | solution.py:18
  177.2 5.8 %copy-start.10 = (s32[4,256]{1,0:T(4,128)S(1)}, s32[4,256]{1,0:T(4,128)}, u32[]{:S(2)}) copy-start(s32[4,256]{1,0:T(4,128)} %param.18) | copy-start | bytes 12292
  177.3 10.9 %collective-permute-start.8 = (f32[8,3,1,4096]{3,0,2,1:T(8,128)S(1)}, f32[8,3,1,4096]{3,0,2,1:T(8,128)S(1)}, u32[]{:S(2)}, u32[]{:S(2)}) collective-permute-start(f32[8,3,1,4096]{3,0,2,1:T(8,128)S(1)} %get-tuple-element.37), channel_id=1, source_target_pairs={{0,1},{1,2},{2,3},{3,4},{4,5},{5,6},{6,7},{7,8},{8,9},{9,10},{10,1... | collective-permute-start | bytes 1179656 | tf_op jit(solution)/shard_map/ppermute | solution.py:18
  177.4 10.9 %collective-permute-start.9 = (f32[8,3,1,4096]{3,0,2,1:T(8,128)S(1)}, f32[8,3,1,4096]{3,0,2,1:T(8,128)S(1)}, u32[]{:S(2)}, u32[]{:S(2)}) collective-permute-start(f32[8,3,1,4096]{3,0,2,1:T(8,128)S(1)} %get-tuple-element.38), channel_id=1, source_target_pairs={{1,0},{2,1},{3,2},{4,3},{5,4},{6,5},{7,6},{8,7},{9,8},{10,9},{11,1... | collective-permute-start | bytes 1179656 | tf_op jit(solution)/shard_map/ppermute | solution.py:21
  195.1 19.7 %copy-start.1 = (f32[8,16,4096]{2,0,1:T(8,128)}, f32[8,16,4096]{2,0,1:T(8,128)S(1)}, u32[]{:S(2)}) copy-start(f32[8,16,4096]{2,0,1:T(8,128)S(1)} %fusion.36) | copy-start | bytes 6291460
  195.2 8.1 %collective-permute-start.10 = (f32[8,1,4096]{2,0,1:T(8,128)S(1)}, f32[8,1,4096]{2,0,1:T(8,128)S(1)}, u32[]{:S(2)}, u32[]{:S(2)}) collective-permute-start(f32[8,1,4096]{2,0,1:T(8,128)S(1)} %get-tuple-element.90), channel_id=1, source_target_pairs={{1,0},{2,1},{3,2},{4,3},{5,4},{6,5},{7,6},{8,7},{9,8},{10,9},{11,1... | collective-permute-start | bytes 393224 | tf_op jit(solution)/shard_map/ppermute | solution.py:21
  200.8 8.0 %collective-permute-start.11 = (f32[8,1,4096]{2,0,1:T(8,128)S(1)}, f32[8,1,4096]{2,0,1:T(8,128)S(1)}, u32[]{:S(2)}, u32[]{:S(2)}) collective-permute-start(f32[8,1,4096]{2,0,1:T(8,128)S(1)} %get-tuple-element.89), channel_id=1, source_target_pairs={{0,1},{1,2},{2,3},{3,4},{4,5},{5,6},{6,7},{7,8},{8,9},{9,10},{10,1... | collective-permute-start | bytes 393224 | tf_op jit(solution)/shard_map/ppermute | solution.py:18
  214.9 7.2 %copy-start.9 = (f32[4,256]{1,0:T(4,128)S(1)}, f32[4,256]{1,0:T(4,128)}, u32[]{:S(2)}) copy-start(f32[4,256]{1,0:T(4,128)} %param.21) | copy-start | bytes 12292
  216.4 94.4 %collective-permute-start.12 = (f32[8,3,1,4096]{3,0,2,1:T(8,128)}, f32[8,3,1,4096]{3,0,2,1:T(8,128)S(1)}, u32[]{:S(2)}, u32[]{:S(2)}) collective-permute-start(f32[8,3,1,4096]{3,0,2,1:T(8,128)} %get-tuple-element.35), channel_id=1, source_target_pairs={{0,1},{1,2},{2,3},{3,4},{4,5},{5,6},{6,7},{7,8},{8,9},{9,10},{10,1... | collective-permute-start | bytes 1179656 | tf_op jit(solution)/shard_map/ppermute | solution.py:18
  216.4 94.4 %collective-permute-start.13 = (f32[8,3,1,4096]{3,0,2,1:T(8,128)}, f32[8,3,1,4096]{3,0,2,1:T(8,128)}, u32[]{:S(2)}, u32[]{:S(2)}) collective-permute-start(f32[8,3,1,4096]{3,0,2,1:T(8,128)} %get-tuple-element.36), channel_id=1, source_target_pairs={{1,0},{2,1},{3,2},{4,3},{5,4},{6,5},{7,6},{8,7},{9,8},{10,9},{11,1... | collective-permute-start | bytes 1179656 | tf_op jit(solution)/shard_map/ppermute | solution.py:21
  251.0 29.8 %copy-start.2 = (f32[8,16,4096]{2,0,1:T(8,128)S(1)}, f32[8,16,4096]{2,0,1:T(8,128)}, u32[]{:S(2)}) copy-start(f32[8,16,4096]{2,0,1:T(8,128)} %copy-done.1) | copy-start | bytes 6291460
  316.2 29.0 %copy-start.8 = (f32[4,256]{1,0:T(4,128)S(1)}, f32[4,256]{1,0:T(4,128)}, u32[]{:S(2)}) copy-start(f32[4,256]{1,0:T(4,128)} %param.19) | copy-start | bytes 12292
  331.8 43.5 %copy-start.12 = (f32[4,256]{1,0:T(4,128)S(1)}, f32[4,256]{1,0:T(4,128)}, u32[]{:S(2)}) copy-start(f32[4,256]{1,0:T(4,128)} %param.20) | copy-start | bytes 12292
  345.2 96.5 %copy-start.15 = (f32[64]{0:T(128)S(1)}, f32[64]{0:T(128)}, u32[]{:S(2)}) copy-start(f32[64]{0:T(128)} %param.14) | copy-start | bytes 772
  (7 other events, 25.0 us)
Sparse Core Ops, SparseCore 0:
  20.1 78.3 all-reduce.2
where the time goes:
time: 459 us; the launch traced here: 450 us
  local copies, waits for them, and re-layouts  139 us (30%)
  waiting for transfers between devices  113 us (25%)
  blocking collectives  93.4 us (20%)
  starting transfers between devices  39.3 us (9%)
  other arithmetic  38.2 us (8%)
  between operations  15.1 us (3%)
  matrix products  12 us (3%)
    psum x1, waiting for transfers between devices, body(): increment = lax.psum(partial_value, 'mem')  78.6 us
    psum x1, blocking collectives, body(): gram, pull = lax.psum((gram, pull), 'sp')  65 us
    sub x4, local copies, waits for them, and re-layouts, height_update(): height[:, 1:-1]  63.1 us
    gather x4, local copies, waits for them, and re-layouts, observe(): picked = jnp.take(flat, flat_index, axis=1)  54.6 us
    ppermute x7, starting transfers between devices, padded_2(): lax.ppermute(lax.slice_in_dim(block, 0, width, axis=dim), axis, backward)  39 us
    ppermute x7, waiting for transfers between devices, padded_2(): lax.ppermute(lax.slice_in_dim(block, block.shape[dim] - width, None, axis...  31.4 us
    all_gather x1, blocking collectives, body(): gathered = lax.all_gather(own_obs, 'mem', axis=0, tiled=True)  28.4 us
    another operation x6, other arithmetic, momentum_update(): return jnp.stack([fresh[:, 1:-1], new_u, new_v], axis=1)  15.1 us
  transfers between devices with their start and end apart: 15, of which 10 were waited for; matrix products, arithmetic and copies ran while one was open for 21% of the time, Pallas kernels for 0%

commit v1 on v0

--- a/solution.py
+++ b/solution.py
@@ -94,7 +94,9 @@
         state = momentum_update(fresh_pad, padded[:, 1], padded[:, 2])
         seen.append(observe(state[:, 0], flat_index, obs_weight))
     own_obs = jnp.stack(seen, axis=1)
-    gathered = lax.all_gather(own_obs, "mem", axis=0, tiled=True)
+    gathered = jnp.concatenate(
+        lax.all_to_all(jnp.stack([own_obs] * lax.axis_size("mem")), "mem", 0, 0), axis=0
+    )
     mean_obs = jnp.mean(gathered, axis=0)
     obs_anom = (own_obs - mean_obs) / perturb
     flat_anom = ((gathered - mean_obs) / perturb).reshape(total, -1)

time: 459 us -> 439 us (0.956)
  blocking collectives: 93.4 us -> 65 us
  waiting for transfers between devices: 113 us -> 122 us
    all_gather x1 -> x0, blocking collectives: 28.4 us -> none  [body(): gathered = lax.all_gather(own_obs, 'mem', axis=0, tiled=True)]
    all_to_all x0 -> x1, waiting for transfers between devices: none -> 7.27 us  [body(): lax.all_to_all(jnp.stack([own_obs] * lax.axis_size('mem')), 'mem', 0, 0)]
  transfers between devices with their start and end apart: 15 -> 16, of which waited for: 10 -> 12; matrix products, arithmetic and copies ran while one was open for 21% -> 22% of each run, Pallas kernels for 0% -> 0%
where the time goes in v1:
time: 439 us; the launch traced here: 431 us
  local copies, waits for them, and re-layouts  135 us (31%)
  waiting for transfers between devices  122 us (28%)
  blocking collectives  65 us (15%)
  starting transfers between devices  42.8 us (10%)
  other arithmetic  38.1 us (9%)
  between operations  15.2 us (3%)
  matrix products  12 us (3%)
    psum x1, waiting for transfers between devices, body(): increment = lax.psum(partial_value, 'mem')  78.6 us
    psum x1, blocking collectives, body(): gram, pull = lax.psum((gram, pull), 'sp')  65 us
    sub x4, local copies, waits for them, and re-layouts, height_update(): height[:, 1:-1]  63.3 us
    gather x4, local copies, waits for them, and re-layouts, observe(): picked = jnp.take(flat, flat_index, axis=1)  54.6 us
    ppermute x7, starting transfers between devices, padded_2(): lax.ppermute(lax.slice_in_dim(block, 0, width, axis=dim), axis, backward)  39 us
    ppermute x7, waiting for transfers between devices, padded_2(): lax.ppermute(lax.slice_in_dim(block, block.shape[dim] - width, None, axis...  32.3 us
    another operation x6, other arithmetic, momentum_update(): return jnp.stack([fresh[:, 1:-1], new_u, new_v], axis=1)  15.1 us
    slice x21, local copies, waits for them, and re-layouts, col_diff(): return (jnp.roll(a, -1, axis=-1) - jnp.roll(a, 1, axis=-1)) * 0.5  11.5 us
  transfers between devices with their start and end apart: 16, of which 12 were waited for; matrix products, arithmetic and copies ran while one was open for 22% of the time, Pallas kernels for 0%

profile of v1, /device:TPU:0, one launch (start us, length us, event | category | flops | bytes accessed | tf_op | source)
XLA Modules:
  0.0 430.7 jit_solution(18393997282913918250)
XLA Ops:
  7.2 11.4 %fusion = f32[1,3,16,4096]{3,0,2,1:T(1,128)S(1)} fusion(f32[8,3,16,4096]{3,2,1,0:T(8,128)} %param.12, f32[64]{0:T(128)} %param.14, s32[]{:T(128)S(6)} %select_n.17), kind=kOutput, calls=%fused_computation.9 | convolution fusion | flops 18874368 | bytes 7078148 | tf_op jit(solution)/shard_map/dot_general | solution.py:82
  20.0 78.6 %all-reduce.3.cloned.1.call-done = f32[3,16,4096]{2,1,0:T(8,128)} async-done(((f32[3,16,4096]{2,1,0:T(8,128)}), f32[3,16,4096]{2,1,0:T(8,128)}) %all-reduce.3.cloned.1.call-update) | async-done | bytes 786448 | tf_op jit(solution)/shard_map/psum | solution.py:83
  99.8 7.0 %multiply_add_fusion = f32[8,3,16,4096]{3,0,2,1:T(8,128)S(1)} fusion(f32[8,3,16,4096]{3,2,1,0:T(8,128)} %param.12, f32[3,16,4096]{2,1,0:T(8,128)S(1)} %add.97), kind=kLoop, calls=%fused_computation.8 | loop fusion | flops 3145728 | bytes 13369344 | tf_op jit(solution)/shard_map/add | solution.py:85
  106.9 5.5 %collective-permute-start.1 = (f32[8,3,1,4096]{3,0,2,1:T(8,128)S(1)}, f32[8,3,1,4096]{3,0,2,1:T(8,128)S(1)}, u32[]{:S(2)}, u32[]{:S(2)}) collective-permute-start(f32[8,3,1,4096]{3,0,2,1:T(8,128)S(1)} %get-tuple-element.45), channel_id=1, source_target_pairs={{1,0},{2,1},{3,2},{4,3},{5,4},{6,5},{7,6},{8,7},{9,8},{10,9},{11,1... | collective-permute-start | bytes 1179656 | tf_op jit(solution)/shard_map/ppermute | solution.py:21
  112.4 5.3 %collective-permute-done = f32[8,3,1,4096]{3,0,2,1:T(8,128)S(1)} collective-permute-done((f32[8,3,1,4096]{3,0,2,1:T(8,128)S(1)}, f32[8,3,1,4096]{3,0,2,1:T(8,128)S(1)}, u32[]{:S(2)}, u32[]{:S(2)}) %collective-permute-start) | collective-permute-done | bytes 393248 | tf_op jit(solution)/shard_map/ppermute | solution.py:18
  121.3 5.6 %collective-permute-start.2 = (f32[8,1,4096]{2,0,1:T(8,128)S(1)}, f32[8,1,4096]{2,0,1:T(8,128)S(1)}, u32[]{:S(2)}, u32[]{:S(2)}) collective-permute-start(f32[8,1,4096]{2,0,1:T(8,128)S(1)} %get-tuple-element.97), channel_id=1, source_target_pairs={{1,0},{2,1},{3,2},{4,3},{5,4},{6,5},{7,6},{8,7},{9,8},{10,9},{11,1... | collective-permute-start | bytes 393224 | tf_op jit(solution)/shard_map/ppermute | solution.py:21
  129.4 5.5 %collective-permute-done.3 = f32[8,1,4096]{2,0,1:T(8,128)S(1)} collective-permute-done((f32[8,1,4096]{2,0,1:T(8,128)S(1)}, f32[8,1,4096]{2,0,1:T(8,128)S(1)}, u32[]{:S(2)}, u32[]{:S(2)}) %collective-permute-start.3) | collective-permute-done | bytes 131104 | tf_op jit(solution)/shard_map/ppermute | solution.py:18
  141.1 5.5 %collective-permute-start.5 = (f32[8,3,1,4096]{3,0,2,1:T(8,128)S(1)}, f32[8,3,1,4096]{3,0,2,1:T(8,128)S(1)}, u32[]{:S(2)}, u32[]{:S(2)}) collective-permute-start(f32[8,3,1,4096]{3,0,2,1:T(8,128)S(1)} %get-tuple-element.43), channel_id=1, source_target_pairs={{1,0},{2,1},{3,2},{4,3},{5,4},{6,5},{7,6},{8,7},{9,8},{10,9},{11,1... | collective-permute-start | bytes 1179656 | tf_op jit(solution)/shard_map/ppermute | solution.py:21
  156.7 5.6 %collective-permute-start.6 = (f32[8,1,4096]{2,0,1:T(8,128)S(1)}, f32[8,1,4096]{2,0,1:T(8,128)S(1)}, u32[]{:S(2)}, u32[]{:S(2)}) collective-permute-start(f32[8,1,4096]{2,0,1:T(8,128)S(1)} %get-tuple-element.95), channel_id=1, source_target_pairs={{1,0},{2,1},{3,2},{4,3},{5,4},{6,5},{7,6},{8,7},{9,8},{10,9},{11,1... | collective-permute-start | bytes 393224 | tf_op jit(solution)/shard_map/ppermute | solution.py:21
  164.8 5.5 %collective-permute-done.7 = f32[8,1,4096]{2,0,1:T(8,128)S(1)} collective-permute-done((f32[8,1,4096]{2,0,1:T(8,128)S(1)}, f32[8,1,4096]{2,0,1:T(8,128)S(1)}, u32[]{:S(2)}, u32[]{:S(2)}) %collective-permute-start.7) | collective-permute-done | bytes 131104 | tf_op jit(solution)/shard_map/ppermute | solution.py:18
  176.5 5.6 %collective-permute-start.9 = (f32[8,3,1,4096]{3,0,2,1:T(8,128)S(1)}, f32[8,3,1,4096]{3,0,2,1:T(8,128)S(1)}, u32[]{:S(2)}, u32[]{:S(2)}) collective-permute-start(f32[8,3,1,4096]{3,0,2,1:T(8,128)S(1)} %get-tuple-element.41), channel_id=1, source_target_pairs={{1,0},{2,1},{3,2},{4,3},{5,4},{6,5},{7,6},{8,7},{9,8},{10,9},{11,1... | collective-permute-start | bytes 1179656 | tf_op jit(solution)/shard_map/ppermute | solution.py:21
  192.2 5.6 %collective-permute-start.10 = (f32[8,1,4096]{2,0,1:T(8,128)S(1)}, f32[8,1,4096]{2,0,1:T(8,128)S(1)}, u32[]{:S(2)}, u32[]{:S(2)}) collective-permute-start(f32[8,1,4096]{2,0,1:T(8,128)S(1)} %get-tuple-element.93), channel_id=1, source_target_pairs={{1,0},{2,1},{3,2},{4,3},{5,4},{6,5},{7,6},{8,7},{9,8},{10,9},{11,1... | collective-permute-start | bytes 393224 | tf_op jit(solution)/shard_map/ppermute | solution.py:21
  200.3 5.5 %collective-permute-done.11 = f32[8,1,4096]{2,0,1:T(8,128)S(1)} collective-permute-done((f32[8,1,4096]{2,0,1:T(8,128)S(1)}, f32[8,1,4096]{2,0,1:T(8,128)S(1)}, u32[]{:S(2)}, u32[]{:S(2)}) %collective-permute-start.11) | collective-permute-done | bytes 131104 | tf_op jit(solution)/shard_map/ppermute | solution.py:18
  213.4 5.6 %collective-permute-start.13 = (f32[8,3,1,4096]{3,0,2,1:T(8,128)}, f32[8,3,1,4096]{3,0,2,1:T(8,128)}, u32[]{:S(2)}, u32[]{:S(2)}) collective-permute-start(f32[8,3,1,4096]{3,0,2,1:T(8,128)} %get-tuple-element.39), channel_id=1, source_target_pairs={{1,0},{2,1},{3,2},{4,3},{5,4},{6,5},{7,6},{8,7},{9,8},{10,9},{11,1... | collective-permute-start | bytes 1179656 | tf_op jit(solution)/shard_map/ppermute | solution.py:21
  219.1 15.6 %copy.39 = f32[8,16,4096]{0,2,1:T(8,128)} copy(f32[8,16,4096]{2,0,1:T(8,128)S(1)} %fusion.94) | data formatting | bytes 4194304 | tf_op jit(solution)/shard_map/sub | solution.py:36
  234.7 13.3 %gather_fusion = f32[1024,8]{1,0:T(8,128)S(1)} fusion(f32[8,65536]{0,1:T(8,128)} %bitcast.129, s32[1024]{0:T(1024)S(1)} %broadcast_clamp_fusion), kind=kCustom, calls=%fused_computation.clone | custom fusion | bytes 69632 | tf_op jit(solution)/shard_map/jit(_take)/gather | solution.py:61
  248.1 16.5 %copy.41 = f32[8,16,4096]{0,2,1:T(8,128)} copy(f32[8,16,4096]{2,0,1:T(8,128)} %copy-done) | data formatting | bytes 4194304 | tf_op jit(solution)/shard_map/sub | solution.py:36
  264.6 13.3 %gather_fusion.1 = f32[1024,8]{1,0:T(8,128)S(1)} fusion(f32[8,65536]{0,1:T(8,128)} %bitcast.130, s32[1024]{0:T(1024)S(1)} %broadcast_clamp_fusion), kind=kCustom, calls=%fused_computation.1.clone | custom fusion | bytes 69632 | tf_op jit(solution)/shard_map/jit(_take)/gather | solution.py:61
  277.9 15.6 %copy.43 = f32[8,16,4096]{0,2,1:T(8,128)} copy(f32[8,16,4096]{2,0,1:T(8,128)S(1)} %copy-done.2) | data formatting | bytes 4194304 | tf_op jit(solution)/shard_map/sub | solution.py:36
  293.5 14.6 %gather_fusion.2 = f32[1024,8]{1,0:T(8,128)} fusion(f32[8,65536]{0,1:T(8,128)} %bitcast.131, s32[1024]{0:T(1024)S(1)} %broadcast_clamp_fusion), kind=kCustom, calls=%fused_computation.2.clone | custom fusion | bytes 69632 | tf_op jit(solution)/shard_map/jit(_take)/gather | solution.py:61
  313.5 15.6 %copy.45 = f32[8,16,4096]{0,2,1:T(8,128)} copy(f32[8,16,4096]{2,0,1:T(8,128)S(1)} %fusion.7) | data formatting | bytes 4194304 | tf_op jit(solution)/shard_map/sub | solution.py:36
  329.1 13.3 %gather_fusion.3 = f32[1024,8]{1,0:T(8,128)S(1)} fusion(f32[8,65536]{0,1:T(8,128)} %bitcast.128, s32[1024]{0:T(1024)S(1)} %broadcast_clamp_fusion), kind=kCustom, calls=%fused_computation.3.clone | custom fusion | bytes 69632 | tf_op jit(solution)/shard_map/jit(_take)/gather | solution.py:61
  348.5 7.3 %all-to-all-done = f32[8,8,4,256]{3,1,2,0:T(8,128)S(1)} async-done(((f32[8,8,4,256]{3,1,2,0:T(8,128)}), f32[8,8,4,256]{3,1,2,0:T(8,128)S(1)}, u32[]{:S(2)}, u32[]{:S(2)}) %all-to-all-start) | async-done | bytes 262176 | tf_op jit(solution)/shard_map/all_to_all | solution.py:98
  356.5 65.0 %all-reduce = (f32[64]{0:T(128)S(1)}, f32[64,64]{1,0:T(8,128)S(1)}) all-reduce(f32[64]{0:T(128)S(1)} %convolution_bitcast_fusion, f32[64,64]{1,0:T(8,128)S(1)} %fusion.131), channel_id=1, replica_groups=mesh['mem'=8,'sp'=16] {'sp'}, use_global_device_ids=true, to_apply=%region_6.8 | all-reduce | flops 4160 | bytes 33280 | tf_op jit(solution)/shard_map/psum | solution.py:107
  (124 shorter events, 67.6 us)
Async XLA Ops:
  7.2 91.4 %all-reduce.3.cloned.1.call-start = ((), (), s32[]{:S(2)}) async-start(), calls=%async_computation.1 | async-start | bytes 1572864 | tf_op jit(solution)/shard_map/psum | solution.py:83
  18.6 80.0 %copy-start.5 = (f32[3,16,4096]{2,1,0:T(8,128)S(1)}, f32[3,16,4096]{2,1,0:T(8,128)}, u32[]{:S(2)}) copy-start(f32[3,16,4096]{2,1,0:T(8,128)} %param.13) | copy-start | bytes 2359300
  106.8 10.9 %collective-permute-start = (f32[8,3,1,4096]{3,0,2,1:T(8,128)S(1)}, f32[8,3,1,4096]{3,0,2,1:T(8,128)S(1)}, u32[]{:S(2)}, u32[]{:S(2)}) collective-permute-start(f32[8,3,1,4096]{3,0,2,1:T(8,128)S(1)} %get-tuple-element.44), channel_id=1, source_target_pairs={{0,1},{1,2},{2,3},{3,4},{4,5},{5,6},{6,7},{7,8},{8,9},{9,10},{10,1... | collective-permute-start | bytes 1179656 | tf_op jit(solution)/shard_map/ppermute | solution.py:18
  106.9 10.8 %collective-permute-start.1 = (f32[8,3,1,4096]{3,0,2,1:T(8,128)S(1)}, f32[8,3,1,4096]{3,0,2,1:T(8,128)S(1)}, u32[]{:S(2)}, u32[]{:S(2)}) collective-permute-start(f32[8,3,1,4096]{3,0,2,1:T(8,128)S(1)} %get-tuple-element.45), channel_id=1, source_target_pairs={{1,0},{2,1},{3,2},{4,3},{5,4},{6,5},{7,6},{8,7},{9,8},{10,9},{11,1... | collective-permute-start | bytes 1179656 | tf_op jit(solution)/shard_map/ppermute | solution.py:21
  121.3 8.1 %collective-permute-start.2 = (f32[8,1,4096]{2,0,1:T(8,128)S(1)}, f32[8,1,4096]{2,0,1:T(8,128)S(1)}, u32[]{:S(2)}, u32[]{:S(2)}) collective-permute-start(f32[8,1,4096]{2,0,1:T(8,128)S(1)} %get-tuple-element.97), channel_id=1, source_target_pairs={{1,0},{2,1},{3,2},{4,3},{5,4},{6,5},{7,6},{8,7},{9,8},{10,9},{11,1... | collective-permute-start | bytes 393224 | tf_op jit(solution)/shard_map/ppermute | solution.py:21
  126.8 8.0 %collective-permute-start.3 = (f32[8,1,4096]{2,0,1:T(8,128)S(1)}, f32[8,1,4096]{2,0,1:T(8,128)S(1)}, u32[]{:S(2)}, u32[]{:S(2)}) collective-permute-start(f32[8,1,4096]{2,0,1:T(8,128)S(1)} %get-tuple-element.96), channel_id=1, source_target_pairs={{0,1},{1,2},{2,3},{3,4},{4,5},{5,6},{6,7},{7,8},{8,9},{9,10},{10,1... | collective-permute-start | bytes 393224 | tf_op jit(solution)/shard_map/ppermute | solution.py:18
  141.0 10.9 %collective-permute-start.4 = (f32[8,3,1,4096]{3,0,2,1:T(8,128)S(1)}, f32[8,3,1,4096]{3,0,2,1:T(8,128)S(1)}, u32[]{:S(2)}, u32[]{:S(2)}) collective-permute-start(f32[8,3,1,4096]{3,0,2,1:T(8,128)S(1)} %get-tuple-element.42), channel_id=1, source_target_pairs={{0,1},{1,2},{2,3},{3,4},{4,5},{5,6},{6,7},{7,8},{8,9},{9,10},{10,1... | collective-permute-start | bytes 1179656 | tf_op jit(solution)/shard_map/ppermute | solution.py:18
  141.1 10.8 %collective-permute-start.5 = (f32[8,3,1,4096]{3,0,2,1:T(8,128)S(1)}, f32[8,3,1,4096]{3,0,2,1:T(8,128)S(1)}, u32[]{:S(2)}, u32[]{:S(2)}) collective-permute-start(f32[8,3,1,4096]{3,0,2,1:T(8,128)S(1)} %get-tuple-element.43), channel_id=1, source_target_pairs={{1,0},{2,1},{3,2},{4,3},{5,4},{6,5},{7,6},{8,7},{9,8},{10,9},{11,1... | collective-permute-start | bytes 1179656 | tf_op jit(solution)/shard_map/ppermute | solution.py:21
  156.6 30.7 %copy-start = (f32[8,16,4096]{2,0,1:T(8,128)}, f32[8,16,4096]{2,0,1:T(8,128)S(1)}, u32[]{:S(2)}) copy-start(f32[8,16,4096]{2,0,1:T(8,128)S(1)} %fusion.65) | copy-start | bytes 6291460
  156.7 8.1 %collective-permute-start.6 = (f32[8,1,4096]{2,0,1:T(8,128)S(1)}, f32[8,1,4096]{2,0,1:T(8,128)S(1)}, u32[]{:S(2)}, u32[]{:S(2)}) collective-permute-start(f32[8,1,4096]{2,0,1:T(8,128)S(1)} %get-tuple-element.95), channel_id=1, source_target_pairs={{1,0},{2,1},{3,2},{4,3},{5,4},{6,5},{7,6},{8,7},{9,8},{10,9},{11,1... | collective-permute-start | bytes 393224 | tf_op jit(solution)/shard_map/ppermute | solution.py:21
  162.3 8.0 %collective-permute-start.7 = (f32[8,1,4096]{2,0,1:T(8,128)S(1)}, f32[8,1,4096]{2,0,1:T(8,128)S(1)}, u32[]{:S(2)}, u32[]{:S(2)}) collective-permute-start(f32[8,1,4096]{2,0,1:T(8,128)S(1)} %get-tuple-element.94), channel_id=1, source_target_pairs={{0,1},{1,2},{2,3},{3,4},{4,5},{5,6},{6,7},{7,8},{8,9},{9,10},{10,1... | collective-permute-start | bytes 393224 | tf_op jit(solution)/shard_map/ppermute | solution.py:18
  176.4 10.9 %collective-permute-start.8 = (f32[8,3,1,4096]{3,0,2,1:T(8,128)S(1)}, f32[8,3,1,4096]{3,0,2,1:T(8,128)S(1)}, u32[]{:S(2)}, u32[]{:S(2)}) collective-permute-start(f32[8,3,1,4096]{3,0,2,1:T(8,128)S(1)} %get-tuple-element.40), channel_id=1, source_target_pairs={{0,1},{1,2},{2,3},{3,4},{4,5},{5,6},{6,7},{7,8},{8,9},{9,10},{10,1... | collective-permute-start | bytes 1179656 | tf_op jit(solution)/shard_map/ppermute | solution.py:18
  176.5 10.9 %collective-permute-start.9 = (f32[8,3,1,4096]{3,0,2,1:T(8,128)S(1)}, f32[8,3,1,4096]{3,0,2,1:T(8,128)S(1)}, u32[]{:S(2)}, u32[]{:S(2)}) collective-permute-start(f32[8,3,1,4096]{3,0,2,1:T(8,128)S(1)} %get-tuple-element.41), channel_id=1, source_target_pairs={{1,0},{2,1},{3,2},{4,3},{5,4},{6,5},{7,6},{8,7},{9,8},{10,9},{11,1... | collective-permute-start | bytes 1179656 | tf_op jit(solution)/shard_map/ppermute | solution.py:21
  192.1 19.7 %copy-start.1 = (f32[8,16,4096]{2,0,1:T(8,128)}, f32[8,16,4096]{2,0,1:T(8,128)S(1)}, u32[]{:S(2)}) copy-start(f32[8,16,4096]{2,0,1:T(8,128)S(1)} %fusion.36) | copy-start | bytes 6291460
  192.2 8.1 %collective-permute-start.10 = (f32[8,1,4096]{2,0,1:T(8,128)S(1)}, f32[8,1,4096]{2,0,1:T(8,128)S(1)}, u32[]{:S(2)}, u32[]{:S(2)}) collective-permute-start(f32[8,1,4096]{2,0,1:T(8,128)S(1)} %get-tuple-element.93), channel_id=1, source_target_pairs={{1,0},{2,1},{3,2},{4,3},{5,4},{6,5},{7,6},{8,7},{9,8},{10,9},{11,1... | collective-permute-start | bytes 393224 | tf_op jit(solution)/shard_map/ppermute | solution.py:21
  197.8 8.0 %collective-permute-start.11 = (f32[8,1,4096]{2,0,1:T(8,128)S(1)}, f32[8,1,4096]{2,0,1:T(8,128)S(1)}, u32[]{:S(2)}, u32[]{:S(2)}) collective-permute-start(f32[8,1,4096]{2,0,1:T(8,128)S(1)} %get-tuple-element.92), channel_id=1, source_target_pairs={{0,1},{1,2},{2,3},{3,4},{4,5},{5,6},{6,7},{7,8},{8,9},{9,10},{10,1... | collective-permute-start | bytes 393224 | tf_op jit(solution)/shard_map/ppermute | solution.py:18
  211.9 7.2 %copy-start.8 = (s32[4,256]{1,0:T(4,128)S(1)}, s32[4,256]{1,0:T(4,128)}, u32[]{:S(2)}) copy-start(s32[4,256]{1,0:T(4,128)} %param.18) | copy-start | bytes 12292
  213.4 94.7 %collective-permute-start.12 = (f32[8,3,1,4096]{3,0,2,1:T(8,128)}, f32[8,3,1,4096]{3,0,2,1:T(8,128)S(1)}, u32[]{:S(2)}, u32[]{:S(2)}) collective-permute-start(f32[8,3,1,4096]{3,0,2,1:T(8,128)} %get-tuple-element.38), channel_id=1, source_target_pairs={{0,1},{1,2},{2,3},{3,4},{4,5},{5,6},{6,7},{7,8},{8,9},{9,10},{10,1... | collective-permute-start | bytes 1179656 | tf_op jit(solution)/shard_map/ppermute | solution.py:18
  213.4 94.7 %collective-permute-start.13 = (f32[8,3,1,4096]{3,0,2,1:T(8,128)}, f32[8,3,1,4096]{3,0,2,1:T(8,128)}, u32[]{:S(2)}, u32[]{:S(2)}) collective-permute-start(f32[8,3,1,4096]{3,0,2,1:T(8,128)} %get-tuple-element.39), channel_id=1, source_target_pairs={{1,0},{2,1},{3,2},{4,3},{5,4},{6,5},{7,6},{8,7},{9,8},{10,9},{11,1... | collective-permute-start | bytes 1179656 | tf_op jit(solution)/shard_map/ppermute | solution.py:21
  248.1 29.8 %copy-start.2 = (f32[8,16,4096]{2,0,1:T(8,128)S(1)}, f32[8,16,4096]{2,0,1:T(8,128)}, u32[]{:S(2)}) copy-start(f32[8,16,4096]{2,0,1:T(8,128)} %copy-done.1) | copy-start | bytes 6291460
  313.4 29.0 %copy-start.6 = (f32[4,256]{1,0:T(4,128)S(1)}, f32[4,256]{1,0:T(4,128)}, u32[]{:S(2)}) copy-start(f32[4,256]{1,0:T(4,128)} %param.19) | copy-start | bytes 12292
  342.5 13.3 %copy-start.10 = (f32[4,256]{1,0:T(4,128)S(1)}, f32[4,256]{1,0:T(4,128)}, u32[]{:S(2)}) copy-start(f32[4,256]{1,0:T(4,128)} %param.20) | copy-start | bytes 12292
  343.9 78.3 %copy-start.13 = (f32[64]{0:T(128)S(1)}, f32[64]{0:T(128)}, u32[]{:S(2)}) copy-start(f32[64]{0:T(128)} %param.14) | copy-start | bytes 772
  344.9 10.8 %all-to-all-start = ((f32[8,8,4,256]{3,1,2,0:T(8,128)}), f32[8,8,4,256]{3,1,2,0:T(8,128)S(1)}, u32[]{:S(2)}, u32[]{:S(2)}) async-start(f32[8,8,4,256]{3,1,2,0:T(8,128)} %stack.79), calls=%async_computation | async-start | bytes 524288 | tf_op jit(solution)/shard_map/all_to_all | solution.py:98
  (6 other events, 32.0 us)
Sparse Core Ops, SparseCore 0:
  20.1 78.3 all-reduce.2
